TPU v7x, 512 devices: a whole 4x8x8 slice. The times are simulated.
512 devices in a mesh: tm: 4 (over y_hi, core), pix: 128 (over x, z, y_lo).
Axes of the slice: x: 4, y: 8 (y_hi: 2, y_lo: 4; y = y_hi * 4 + y_lo), z: 8, core: 2. Of those that a mesh axis runs over, the one named last changes fastest.
Arguments:
- activations: bfloat16 [4, 327680, 256], P('tm', 'pix'), may hold values from -6 to 6
- down_weight: bfloat16 [1024, 256], replicated, may hold values from -0.1875 to 0.1875
- down_bias: float32 [256], replicated, may hold values from -3 to 3
- taps: float32 [9, 256], replicated, may hold values from -2 to 2
- point_weight: bfloat16 [256, 256], replicated, may hold values from -0.375 to 0.375
- time_mix: float32 [4, 4, 256], replicated, may hold values from -3 to 3
- edge_rows: int32 [128, 2, 20], P('pix'), may hold values from 0 to 19, as said below
- cotangent: bfloat16 [4, 81920, 256], P(None, ('pix', 'tm')), may hold values from -6 to 6
Outputs:
- grad_input: bfloat16 [4, 327680, 256], P('tm', 'pix')
- grad_down: float32 [1024, 256], replicated
- grad_bias: float32 [256], replicated
- grad_taps: float32 [9, 256], replicated
- grad_point: float32 [256, 256], replicated
- grad_mix: float32 [4, 4, 256], replicated
Inputs may be any that keep to these rules, and one draw needn't show every extreme that they name: Each edge_rows[t, e] is either 0, 1, .., 19 or its reversal; edge_rows[t, 1] equals edge_rows[(t + 1) mod 128, 0].
All inputs are finite; a program needn't handle non-finite values.
Results may differ from a plain program's by a relative error of at most 0.014.
Values may be sent and summed in bfloat16 or wider, within the bound.
No kernel may reach another device: no remote copies, remote signals or barrier semaphores. Data moves between devices by JAX's collectives and lax.ppermute only.
A program may use at most 64 MiB of HBM per device.

v0:
```python
import math
import jax
import jax.numpy as jnp
from jax import lax
from jax.sharding import Mesh, PartitionSpec as P

C = 256
TR = 20
TC = 32
TM = ("yh", "core")
PIX = ("x", "z", "yl")
RING = ("yh", "yl")
SUM_ROWS = 1306
PAD_ROWS = 1536


def padded_2(cells, sides, width):
    for axis, dim in sides:
        count = lax.axis_size(axis)
        head = lax.slice_in_dim(cells, 0, width, axis=dim)
        tail = lax.slice_in_dim(cells, cells.shape[dim] - width, cells.shape[dim], axis=dim)
        cells = jnp.concatenate(
            [
                lax.ppermute(tail, axis, [(i, (i + 1) % count) for i in range(count)]),
                cells,
                lax.ppermute(head, axis, [((i + 1) % count, i) for i in range(count)]),
            ],
            axis=dim,
        )
    return cells


def scatter_sum(rows, axis):
    count = lax.axis_size(axis)
    low = rows.astype(jnp.bfloat16).reshape(count, rows.shape[0] // count, C)
    got = lax.all_to_all(low, axis, split_axis=0, concat_axis=0, tiled=True)
    return jnp.sum(got.astype(jnp.float32), axis=0)


def copies(rows, axis):
    count = lax.axis_size(axis)
    wide = jnp.broadcast_to(rows[None], (count,) + rows.shape)
    return lax.all_to_all(wide, axis, split_axis=0, concat_axis=0, tiled=True)


def sum_over_devices(parts):
    half = PAD_ROWS // 2
    core = lax.axis_index("core")
    keep = lax.dynamic_slice_in_dim(parts, core * half, half, axis=0)
    send = lax.dynamic_slice_in_dim(parts, (1 - core) * half, half, axis=0)
    got = lax.ppermute(send.astype(jnp.bfloat16), "core", [(0, 1), (1, 0)])
    rows = keep + got.astype(jnp.float32)
    rows = scatter_sum(rows, "x")
    rows = scatter_sum(rows, "z")
    rows = jnp.sum(copies(rows.astype(jnp.bfloat16), RING).astype(jnp.float32), axis=0)
    rows = rows.astype(jnp.bfloat16)
    rows = copies(rows, "z").reshape(-1, C)
    rows = copies(rows, "x").reshape(-1, C)
    rows = lax.all_gather(rows, "core", axis=0, tiled=True)
    return rows.astype(jnp.float32)


def on_device(
    activations, down_weight, down_bias, taps, point_weight, time_mix, edge_rows, cotangent
):
    frames = lax.axis_size(TM)
    tiles = lax.axis_size(PIX)
    pixels = TR * TC
    scale = 1.0 / math.sqrt(frames * tiles * pixels)
    rows_in = activations.reshape(pixels, 4 * C)
    preact = jnp.dot(rows_in, down_weight, preferred_element_type=jnp.float32) + down_bias
    pooled = jax.nn.silu(preact).astype(jnp.bfloat16)
    tile_grid = pooled.reshape(1, TR, TC, C)
    padded = padded_2(tile_grid, ((PIX, 2),), 1)
    west_map = edge_rows[0, 0]
    east_map = edge_rows[0, 1]
    west_col = jnp.take(padded[0, :, 0, :], west_map, axis=0)
    east_col = jnp.take(padded[0, :, TC + 1, :], east_map, axis=0)
    widened = jnp.concatenate([west_col[:, None, :], tile_grid[0], east_col[:, None, :]], axis=1)
    widened = jnp.pad(widened, ((1, 1), (0, 0), (0, 0)))
    spread = jnp.zeros((TR, TC, C), jnp.float32)
    for row_off in range(3):
        for col_off in range(3):
            spread = (
                spread
                + taps[row_off * 3 + col_off]
                * widened[row_off : row_off + TR, col_off : col_off + TC, :]
            )
    spread_low = spread.astype(jnp.bfloat16).reshape(pixels, C)
    mixed_in = (
        pooled.astype(jnp.float32)
        + jnp.dot(spread_low, point_weight, preferred_element_type=jnp.float32)
    ).astype(jnp.bfloat16)
    by_pixel = lax.all_to_all(
        mixed_in.reshape(1, pixels, C), TM, split_axis=1, concat_axis=0, tiled=True
    )
    mix_part = jnp.einsum("gpc,fpc->fgc", by_pixel, cotangent, preferred_element_type=jnp.float32)
    cot_f = cotangent.astype(jnp.float32)
    mixed_acc = jnp.zeros((frames, cotangent.shape[1], C), jnp.float32)
    for source in range(frames):
        mixed_acc = mixed_acc + time_mix[source][:, None, :] * cot_f[source][None, :, :]
    mixed_grad = mixed_acc.astype(jnp.bfloat16)
    back_grad = lax.all_to_all(mixed_grad, TM, split_axis=0, concat_axis=1, tiled=True)
    mixed_rows = back_grad.reshape(pixels, C)
    point_part = jnp.dot(spread_low.T, mixed_rows, preferred_element_type=jnp.float32)
    spread_grad = jnp.dot(mixed_rows, point_weight.T, preferred_element_type=jnp.float32).astype(
        jnp.bfloat16
    )
    grad_float = spread_grad.reshape(TR, TC, C).astype(jnp.float32)
    taps_rows = []
    for row_off in range(3):
        for col_off in range(3):
            taps_rows.append(
                jnp.sum(
                    grad_float * widened[row_off : row_off + TR, col_off : col_off + TC, :],
                    axis=(0, 1),
                )
            )
    taps_part = jnp.stack(taps_rows, axis=0)
    grad_padded = jnp.pad(grad_float, ((2, 2), (2, 2), (0, 0)))
    wide_grad = jnp.zeros((TR + 2, TC + 2, C), jnp.float32)
    for row_off in range(3):
        for col_off in range(3):
            wide_grad = (
                wide_grad
                + taps[row_off * 3 + col_off]
                * grad_padded[2 - row_off : 4 - row_off + TR, 2 - col_off : 4 - col_off + TC, :]
            )
    west_back = jnp.take(wide_grad[1 : TR + 1, 0, :], west_map, axis=0)
    east_back = jnp.take(wide_grad[1 : TR + 1, TC + 1, :], east_map, axis=0)
    outgoing = jnp.stack([west_back, east_back], axis=1)
    incoming = padded_2(outgoing.astype(jnp.bfloat16), ((PIX, 1),), 1).astype(outgoing.dtype)
    inner_grad = wide_grad[1 : TR + 1, 1 : TC + 1, :]
    inner_grad = inner_grad.at[:, 0, :].add(incoming[:, 0, :])
    inner_grad = inner_grad.at[:, TC - 1, :].add(incoming[:, 3, :])
    pooled_grad = mixed_rows.astype(jnp.float32) + inner_grad.reshape(pixels, C)
    sigma = jax.nn.sigmoid(preact)
    pre_grad = (pooled_grad * (sigma * (1.0 + preact * (1.0 - sigma)))).astype(jnp.bfloat16)
    bias_part = jnp.sum(pre_grad.astype(jnp.float32), axis=0)
    down_part = jnp.dot(rows_in.T, pre_grad, preferred_element_type=jnp.float32)
    grad_input = jnp.dot(pre_grad, down_weight.T, preferred_element_type=jnp.float32).astype(
        jnp.bfloat16
    )
    parts = jnp.concatenate(
        [
            down_part,
            point_part,
            mix_part.reshape(frames * frames, C),
            taps_part,
            bias_part.reshape(1, C),
            jnp.zeros((PAD_ROWS - SUM_ROWS, C), jnp.float32),
        ],
        axis=0,
    )
    total = sum_over_devices(parts) * scale
    grad_down = total[:1024]
    grad_point = total[1024:1280]
    grad_mix = total[1280:1296].reshape(frames, frames, C)
    grad_taps = total[1296:1305]
    grad_bias = total[1305]
    return (
        grad_input.reshape(1, 4 * pixels, C),
        grad_down,
        grad_bias,
        grad_taps,
        grad_point,
        grad_mix,
    )


def solution(mesh):
    chips = Mesh(mesh.devices.reshape(2, 2, 4, 8, 4), ("yh", "core", "x", "z", "yl"))
    in_specs = (
        P(TM, PIX, None),
        P(),
        P(),
        P(),
        P(),
        P(),
        P(PIX, None, None),
        P(None, PIX + TM, None),
    )
    out_specs = (P(TM, PIX, None), P(), P(), P(), P(), P())
    return jax.shard_map(
        on_device, mesh=chips, in_specs=in_specs, out_specs=out_specs, check_vma=False
    )
```

profile of v0, /device:TPU:1, one launch (start us, length us, event | category | flops | bytes accessed | tf_op | source)
XLA Modules:
  0.0 167.9 jit_solution(9329589787763400051)
XLA Ops:
  3.5 10.3 %all-to-all-start = ((bf16[4,160,256]{2,1,0:T(8,128)(2,1)}), bf16[4,160,256]{2,1,0:T(8,128)(2,1)S(1)}, u32[]{:S(2)}, u32[]{:S(2)}) async-start(bf16[4,160,256]{2,1,0:T(8,128)(2,1)} %add_convert_fusion.1), calls=%async_computation | async-start | bytes 655360 | tf_op jit(solution)/shard_map/all_to_all | solution.py:103
  13.8 9.8 %all-to-all-done = bf16[4,160,256]{2,1,0:T(8,128)(2,1)S(1)} async-done(((bf16[4,160,256]{2,1,0:T(8,128)(2,1)}), bf16[4,160,256]{2,1,0:T(8,128)(2,1)S(1)}, u32[]{:S(2)}, u32[]{:S(2)}) %all-to-all-start) | async-done | bytes 327712 | tf_op jit(solution)/shard_map/all_to_all | solution.py:103
  26.5 11.3 %collective-permute-start.1 = (bf16[20,1,256]{2,0,1:T(8,128)(2,1)S(1)}, bf16[20,1,256]{2,0,1:T(8,128)(2,1)S(1)}, u32[]{:S(2)}, u32[]{:S(2)}) collective-permute-start(bf16[20,1,256]{2,0,1:T(8,128)(2,1)S(1)} %fusion.49), channel_id=1, source_target_pairs={{1,0},{2,1},{3,2},{4,3},{5,4},{6,5},{7,6},{8,7},{9,8},{10,9},{11,1... | collective-permute-start | bytes 30728 | tf_op jit(solution)/shard_map/ppermute | solution.py:26
  38.5 1.9 %collective-permute-start = (bf16[20,1,256]{2,0,1:T(8,128)(2,1)S(1)}, bf16[20,1,256]{2,0,1:T(8,128)(2,1)S(1)}, u32[]{:S(2)}, u32[]{:S(2)}) collective-permute-start(bf16[20,1,256]{2,0,1:T(8,128)(2,1)S(1)} %fusion.48), channel_id=1, source_target_pairs={{0,1},{1,2},{2,3},{3,4},{4,5},{5,6},{6,7},{7,8},{8,9},{9,10},{10,1... | collective-permute-start | bytes 30728 | tf_op jit(solution)/shard_map/ppermute | solution.py:24
  41.5 2.5 %reshape.148 = bf16[640,1024]{1,0:T(8,128)(2,1)S(1)} reshape(bf16[1,2560,256]{2,1,0:T(8,128)(2,1)} %param.16) | data formatting | bytes 2621440 | tf_op jit(solution)/shard_map/reshape | solution.py:70
  45.3 3.7 %collective-permute-done = bf16[20,1,256]{2,0,1:T(8,128)(2,1)S(1)} collective-permute-done((bf16[20,1,256]{2,0,1:T(8,128)(2,1)S(1)}, bf16[20,1,256]{2,0,1:T(8,128)(2,1)S(1)}, u32[]{:S(2)}, u32[]{:S(2)}) %collective-permute-start) | collective-permute-done | bytes 10272 | tf_op jit(solution)/shard_map/ppermute | solution.py:24
  50.8 5.7 %collective-permute-start.3 = (bf16[1,20,1,256]{3,1,2,0:T(8,128)(2,1)S(1)}, bf16[1,20,1,256]{3,1,2,0:T(8,128)(2,1)S(1)}, u32[]{:S(2)}, u32[]{:S(2)}) collective-permute-start(bf16[1,20,1,256]{3,1,2,0:T(8,128)(2,1)S(1)} %copy.128), channel_id=1, source_target_pairs={{1,0},{2,1},{3,2},{4,3},{5,4},{6,5},{7,6},{8,7},{9,8},{10,9},{11,1... | collective-permute-start | bytes 30728 | tf_op jit(solution)/shard_map/ppermute | solution.py:26
  56.5 1.9 %collective-permute-start.2 = (bf16[1,20,1,256]{3,1,2,0:T(8,128)(2,1)S(1)}, bf16[1,20,1,256]{3,1,2,0:T(8,128)(2,1)S(1)}, u32[]{:S(2)}, u32[]{:S(2)}) collective-permute-start(bf16[1,20,1,256]{3,1,2,0:T(8,128)(2,1)S(1)} %copy.127), channel_id=1, source_target_pairs={{0,1},{1,2},{2,3},{3,4},{4,5},{5,6},{6,7},{7,8},{8,9},{9,10},{10,1... | collective-permute-start | bytes 30728 | tf_op jit(solution)/shard_map/ppermute | solution.py:24
  58.4 1.6 convolution_bitcast_fusion
  62.2 4.8 %collective-permute-done.2 = bf16[1,20,1,256]{3,1,2,0:T(8,128)(2,1)S(1)} collective-permute-done((bf16[1,20,1,256]{3,1,2,0:T(8,128)(2,1)S(1)}, bf16[1,20,1,256]{3,1,2,0:T(8,128)(2,1)S(1)}, u32[]{:S(2)}, u32[]{:S(2)}) %collective-permute-start.2) | collective-permute-done | bytes 10272 | tf_op jit(solution)/shard_map/ppermute | solution.py:24
  70.0 3.4 %reduce.8 = bf16[640,256]{1,0:T(8,128)(2,1)} reduce(bf16[640,1,256]{2,1,0:T(2,128)(2,1)S(1)} %bitcast.109, bf16[]{:T(256)} %broadcast.133), dimensions={1}, to_apply=%bitcast.98.reduce_sub_computation | reduce | bytes 655362
  73.4 1.8 %reshape.204 = bf16[4,2,20480]{2,1,0:T(2,128)(2,1)} reshape(bf16[640,256]{1,0:T(8,128)(2,1)} %reduce.8) | data formatting | bytes 655360
  75.1 6.4 %all-to-all-start.1 = ((bf16[4,2,20480]{2,1,0:T(2,128)(2,1)}), bf16[4,2,20480]{2,1,0:T(2,128)(2,1)S(1)}, u32[]{:S(2)}, u32[]{:S(2)}) async-start(bf16[4,2,20480]{2,1,0:T(2,128)(2,1)} %reshape.204), calls=%async_computation.1 | async-start | bytes 655360 | tf_op jit(solution)/shard_map/all_to_all | solution.py:94
  89.6 1.7 %all-to-all-done.1 = bf16[4,2,20480]{2,1,0:T(2,128)(2,1)S(1)} async-done(((bf16[4,2,20480]{2,1,0:T(2,128)(2,1)}), bf16[4,2,20480]{2,1,0:T(2,128)(2,1)S(1)}, u32[]{:S(2)}, u32[]{:S(2)}) %all-to-all-start.1) | async-done | bytes 327712 | tf_op jit(solution)/shard_map/all_to_all | solution.py:94
  96.0 3.0 %concatenate.24 = f32[1536,256]{0,1:T(8,128)S(1)} concatenate(f32[1024,256]{0,1:T(8,128)S(1)} %copy-done.1, f32[256,256]{0,1:T(8,128)S(1)} %copy-done.6, f32[16,256]{0,1:T(8,128)} %copy.113, f32[1,256]{0,1:T(8,128)} %copy.114, f32[1,256]{0,1:T(8,128)} %copy.115, f32[1,256]{0,1:T(8,128)} %copy.116, f32[1,256]{0,1:T(8,128)} %copy.117, f32[1,256]{0,1:T(8,128)} %copy.118, ...), dimensions={0} | concatenate | bytes 3145728 | tf_op jit(solution)/shard_map/concatenate | solution.py:144
  99.1 2.8 %collective-permute-start.4 = (bf16[768,256]{0,1:T(8,128)(2,1)S(1)}, bf16[768,256]{0,1:T(8,128)(2,1)S(1)}, u32[]{:S(2)}, u32[]{:S(2)}) collective-permute-start(bf16[768,256]{0,1:T(8,128)(2,1)S(1)} %dynamic-slice_convert_fusion), channel_id=1, source_target_pairs={{0,128},{128,0},{1,129},{129,1},{2,130},{130,2},{3,131},{131,3},{4... | collective-permute-start | bytes 1179656 | tf_op jit(solution)/shard_map/ppermute | solution.py:51
  103.5 10.2 %all_to_all.46 = bf16[4,192,256]{2,1,0:T(8,128)(2,1)S(1)} all-to-all(bf16[4,192,256]{2,1,0:T(8,128)(2,1)S(1)} %bitcast.111), channel_id=1, replica_groups=mesh['yh'=2,'core'=2,'x'=4,'z'=8,'yl'=4] {'x'}, dimensions={0} | all-to-all | bytes 786432 | tf_op jit(solution)/shard_map/all_to_all | solution.py:36
  113.8 10.2 %all_to_all.47 = bf16[8,24,256]{2,1,0:T(8,128)(2,1)S(1)} all-to-all(bf16[8,24,256]{2,1,0:T(8,128)(2,1)S(1)} %bitcast.116), channel_id=1, replica_groups=mesh['yh'=2,'core'=2,'x'=4,'z'=8,'yl'=4] {'z'}, dimensions={0} | all-to-all | bytes 196608 | tf_op jit(solution)/shard_map/all_to_all | solution.py:36
  124.0 11.8 %all_to_all.48 = bf16[8,24,256]{2,1,0:T(8,128)(2,1)S(1)} all-to-all(bf16[8,24,256]{2,1,0:T(8,128)(2,1)S(1)} %broadcast_in_dim.50), channel_id=1, replica_groups=mesh['yh'=2,'core'=2,'x'=4,'z'=8,'yl'=4] {'yh','yl'}, dimensions={0} | all-to-all | bytes 196608 | tf_op jit(solution)/shard_map/all_to_all | solution.py:43
  135.8 10.0 %all_to_all.49 = bf16[8,24,256]{2,1,0:T(8,128)(2,1)S(1)} all-to-all(bf16[8,24,256]{2,1,0:T(8,128)(2,1)S(1)} %broadcast_in_dim.51), channel_id=1, replica_groups=mesh['yh'=2,'core'=2,'x'=4,'z'=8,'yl'=4] {'z'}, dimensions={0} | all-to-all | bytes 196608 | tf_op jit(solution)/shard_map/all_to_all | solution.py:43
  146.6 3.5 %all-to-all-start.6 = ((bf16[4,192,256]{2,1,0:T(8,128)(2,1)}), bf16[4,192,256]{2,1,0:T(8,128)(2,1)S(1)}, u32[]{:S(2)}, u32[]{:S(2)}) async-start(bf16[4,192,256]{2,1,0:T(8,128)(2,1)} %broadcast_in_dim.53), calls=%async_computation.6 | async-start | bytes 786432 | tf_op jit(solution)/shard_map/all_to_all | solution.py:43
  150.6 1.6 reshape.149
  152.2 4.0 %all-to-all-done.6 = bf16[4,192,256]{2,1,0:T(8,128)(2,1)S(1)} async-done(((bf16[4,192,256]{2,1,0:T(8,128)(2,1)}), bf16[4,192,256]{2,1,0:T(8,128)(2,1)S(1)}, u32[]{:S(2)}, u32[]{:S(2)}) %all-to-all-start.6) | async-done | bytes 393248 | tf_op jit(solution)/shard_map/all_to_all | solution.py:43
  156.2 8.0 %all_gather.3 = bf16[1536,256]{1,0:T(8,128)(2,1)S(1)} all-gather(bf16[768,256]{1,0:T(8,128)(2,1)S(1)} %bitcast.112), channel_id=1, replica_groups=mesh['yh'=2,'core'=2,'x'=4,'z'=8,'yl'=4] {'core'}, dimensions={0}, use_global_device_ids=true | all-gather | bytes 1179648 | tf_op jit(solution)/shard_map/all_gather | solution.py:59
  (99 shorter events, 35.0 us)
Async XLA Ops:
  0.6 49.3 %copy-start = (bf16[1024,256]{1,0:T(8,128)(2,1)S(1)}, bf16[1024,256]{1,0:T(8,128)(2,1)}, u32[]{:S(2)}) copy-start(bf16[1024,256]{1,0:T(8,128)(2,1)} %param.17) | copy-start | bytes 1572868
  2.5 11.3 %copy-start.10 = (s32[1,2,20]{2,1,0:T(2,128)S(1)}, s32[1,2,20]{2,1,0:T(2,128)}, u32[]{:S(2)}) copy-start(s32[1,2,20]{2,1,0:T(2,128)} %param.22) | copy-start | bytes 484
  2.5 11.3 %copy-start.9 = (f32[9,256]{1,0:T(8,128)S(1)}, f32[9,256]{1,0:T(8,128)}, u32[]{:S(2)}) copy-start(f32[9,256]{1,0:T(8,128)} %param.19) | copy-start | bytes 27652
  2.5 21.2 %copy-start.7 = (bf16[256,256]{1,0:T(8,128)(2,1)S(1)}, bf16[256,256]{1,0:T(8,128)(2,1)}, u32[]{:S(2)}) copy-start(bf16[256,256]{1,0:T(8,128)(2,1)} %param.20) | copy-start | bytes 393220
  3.5 20.2 %all-to-all-start = ((bf16[4,160,256]{2,1,0:T(8,128)(2,1)}), bf16[4,160,256]{2,1,0:T(8,128)(2,1)S(1)}, u32[]{:S(2)}, u32[]{:S(2)}) async-start(bf16[4,160,256]{2,1,0:T(8,128)(2,1)} %add_convert_fusion.1), calls=%async_computation | async-start | bytes 655360 | tf_op jit(solution)/shard_map/all_to_all | solution.py:103
  24.3 16.1 %copy-start.3 = (bf16[4,160,256]{2,1,0:T(8,128)(2,1)S(1)}, bf16[4,160,256]{2,1,0:T(8,128)(2,1)}, u32[]{:S(2)}) copy-start(bf16[4,160,256]{2,1,0:T(8,128)(2,1)} %param.23) | copy-start | bytes 983044
  24.9 0.9 copy-start.2
  26.5 18.7 %collective-permute-start.1 = (bf16[20,1,256]{2,0,1:T(8,128)(2,1)S(1)}, bf16[20,1,256]{2,0,1:T(8,128)(2,1)S(1)}, u32[]{:S(2)}, u32[]{:S(2)}) collective-permute-start(bf16[20,1,256]{2,0,1:T(8,128)(2,1)S(1)} %fusion.49), channel_id=1, source_target_pairs={{1,0},{2,1},{3,2},{4,3},{5,4},{6,5},{7,6},{8,7},{9,8},{10,9},{11,1... | collective-permute-start | bytes 30728 | tf_op jit(solution)/shard_map/ppermute | solution.py:26
  38.5 10.4 %collective-permute-start = (bf16[20,1,256]{2,0,1:T(8,128)(2,1)S(1)}, bf16[20,1,256]{2,0,1:T(8,128)(2,1)S(1)}, u32[]{:S(2)}, u32[]{:S(2)}) collective-permute-start(bf16[20,1,256]{2,0,1:T(8,128)(2,1)S(1)} %fusion.48), channel_id=1, source_target_pairs={{0,1},{1,2},{2,3},{3,4},{4,5},{5,6},{6,7},{7,8},{8,9},{9,10},{10,1... | collective-permute-start | bytes 30728 | tf_op jit(solution)/shard_map/ppermute | solution.py:24
  44.0 5.9 %copy-start.11 = (f32[256]{0:T(256)S(1)}, f32[256]{0:T(256)}, u32[]{:S(2)}) copy-start(f32[256]{0:T(256)} %param.18) | copy-start | bytes 3076
  50.8 9.3 %copy-start.4 = (bf16[640,256]{1,0:T(8,128)(2,1)}, bf16[640,256]{1,0:T(8,128)(2,1)S(1)}, u32[]{:S(2)}) copy-start(bf16[640,256]{1,0:T(8,128)(2,1)S(1)} %get-tuple-element.53) | copy-start | bytes 983044
  50.8 10.8 %collective-permute-start.3 = (bf16[1,20,1,256]{3,1,2,0:T(8,128)(2,1)S(1)}, bf16[1,20,1,256]{3,1,2,0:T(8,128)(2,1)S(1)}, u32[]{:S(2)}, u32[]{:S(2)}) collective-permute-start(bf16[1,20,1,256]{3,1,2,0:T(8,128)(2,1)S(1)} %copy.128), channel_id=1, source_target_pairs={{1,0},{2,1},{3,2},{4,3},{5,4},{6,5},{7,6},{8,7},{9,8},{10,9},{11,1... | collective-permute-start | bytes 30728 | tf_op jit(solution)/shard_map/ppermute | solution.py:26
  56.5 10.5 %collective-permute-start.2 = (bf16[1,20,1,256]{3,1,2,0:T(8,128)(2,1)S(1)}, bf16[1,20,1,256]{3,1,2,0:T(8,128)(2,1)S(1)}, u32[]{:S(2)}, u32[]{:S(2)}) collective-permute-start(bf16[1,20,1,256]{3,1,2,0:T(8,128)(2,1)S(1)} %copy.127), channel_id=1, source_target_pairs={{0,1},{1,2},{2,3},{3,4},{4,5},{5,6},{6,7},{7,8},{8,9},{9,10},{10,1... | collective-permute-start | bytes 30728 | tf_op jit(solution)/shard_map/ppermute | solution.py:24
  75.1 16.2 %all-to-all-start.1 = ((bf16[4,2,20480]{2,1,0:T(2,128)(2,1)}), bf16[4,2,20480]{2,1,0:T(2,128)(2,1)S(1)}, u32[]{:S(2)}, u32[]{:S(2)}) async-start(bf16[4,2,20480]{2,1,0:T(2,128)(2,1)} %reshape.204), calls=%async_computation.1 | async-start | bytes 655360 | tf_op jit(solution)/shard_map/all_to_all | solution.py:94
  89.6 3.1 %copy-start.8 = (bf16[4,160,256]{1,0,2:T(4,128)(2,1)S(1)}, bf16[4,160,256]{1,0,2:T(4,128)(2,1)}, u32[]{:S(2)}) copy-start(bf16[4,160,256]{1,0,2:T(4,128)(2,1)} %copy.110) | copy-start | bytes 983044
  92.8 3.3 %copy-start.1 = (f32[1024,256]{0,1:T(8,128)S(1)}, f32[1024,256]{0,1:T(8,128)}, u32[]{:S(2)}) copy-start(f32[1024,256]{0,1:T(8,128)} %convolution_bitcast_fusion) | copy-start | bytes 3145732
  92.8 3.3 %copy-start.6 = (f32[256,256]{0,1:T(8,128)S(1)}, f32[256,256]{0,1:T(8,128)}, u32[]{:S(2)}) copy-start(f32[256,256]{0,1:T(8,128)} %fusion.53) | copy-start | bytes 786436
  99.1 4.1 %collective-permute-start.4 = (bf16[768,256]{0,1:T(8,128)(2,1)S(1)}, bf16[768,256]{0,1:T(8,128)(2,1)S(1)}, u32[]{:S(2)}, u32[]{:S(2)}) collective-permute-start(bf16[768,256]{0,1:T(8,128)(2,1)S(1)} %dynamic-slice_convert_fusion), channel_id=1, source_target_pairs={{0,128},{128,0},{1,129},{129,1},{2,130},{130,2},{3,131},{131,3},{4... | collective-permute-start | bytes 1179656 | tf_op jit(solution)/shard_map/ppermute | solution.py:51
  113.7 36.3 %copy-start.5 = (bf16[640,256]{1,0:T(8,128)(2,1)S(1)}, bf16[640,256]{1,0:T(8,128)(2,1)}, u32[]{:S(2)}) copy-start(bf16[640,256]{1,0:T(8,128)(2,1)} %copy-done.4) | copy-start | bytes 983044
  146.6 9.7 %all-to-all-start.6 = ((bf16[4,192,256]{2,1,0:T(8,128)(2,1)}), bf16[4,192,256]{2,1,0:T(8,128)(2,1)S(1)}, u32[]{:S(2)}, u32[]{:S(2)}) async-start(bf16[4,192,256]{2,1,0:T(8,128)(2,1)} %broadcast_in_dim.53), calls=%async_computation.6 | async-start | bytes 786432 | tf_op jit(solution)/shard_map/all_to_all | solution.py:43
where the time goes:
time: 169 us; the launch traced here: 168 us
  blocking collectives  50.1 us (30%)
  starting transfers between devices  43.8 us (26%)
  local copies, waits for them, and re-layouts  32.7 us (19%)
  waiting for transfers between devices  25.4 us (15%)
  other arithmetic  8.94 us (5%)
  matrix products  5.94 us (4%)
    all_to_all x2, blocking collectives, copies(): return lax.all_to_all(wide, axis, split_axis=0, concat_axis=0, tiled=True)  21.7 us
    all_to_all x2, blocking collectives, scatter_sum(): got = lax.all_to_all(low, axis, split_axis=0, concat_axis=0, tiled=True)  20.4 us
    ppermute x2, starting transfers between devices, padded_2(): lax.ppermute(head, axis, [((i + 1) % count, i) for i in range(count)])  17 us
    all_to_all x1, starting transfers between devices, on_device(): lax.all_to_all(mixed_grad, TM, split_axis=0, concat_axis=1, tiled=True)  10.3 us
    all_to_all x1, waiting for transfers between devices, on_device(): lax.all_to_all(mixed_grad, TM, split_axis=0, concat_axis=1, tiled=True)  9.85 us
    ppermute x2, waiting for transfers between devices, padded_2(): lax.ppermute(tail, axis, [(i, (i + 1) % count) for i in range(count)])  8.5 us
    all_gather x1, blocking collectives, sum_over_devices(): rows = lax.all_gather(rows, 'core', axis=0, tiled=True)  7.95 us
    another operation x9, local copies, waits for them, and re-layouts, on_device(): taps_part = jnp.stack(taps_rows, axis=0)  7.14 us
  transfers between devices with their start and end apart: 8, of which 6 were waited for; matrix products, arithmetic and copies ran while one was open for 12% of the time, Pallas kernels for 0%

commit v1 on v0

--- a/solution.py
+++ b/solution.py
@@ -56,7 +56,9 @@
     rows = rows.astype(jnp.bfloat16)
     rows = copies(rows, "z").reshape(-1, C)
     rows = copies(rows, "x").reshape(-1, C)
-    rows = lax.all_gather(rows, "core", axis=0, tiled=True)
+    rows = jnp.concatenate(
+        lax.all_to_all(jnp.stack([rows] * lax.axis_size("core")), "core", 0, 0), axis=0
+    )
     return rows.astype(jnp.float32)
 
 

time: 169 us -> 170 us (level)
    all_to_all x0 -> x1, blocking collectives: none -> 9.96 us  [sum_over_devices(): lax.all_to_all(jnp.stack([rows] * lax.axis_size('core')), 'core', 0, 0)]
    all_gather x1 -> x0, blocking collectives: 7.95 us -> none  [sum_over_devices(): rows = lax.all_gather(rows, 'core', axis=0, tiled=True)]
    unnamed x31 -> x51, local copies, waits for them, and re-layouts: 4.66 us -> 2.86 us
  transfers between devices with their start and end apart: 8 -> 8, of which waited for: 6 -> 6; matrix products, arithmetic and copies ran while one was open for 12% -> 11% of each run, Pallas kernels for 0% -> 0%
where the time goes in v1:
time: 170 us; the launch traced here: 169 us
  blocking collectives  51.5 us (30%)
  starting transfers between devices  43.8 us (26%)
  local copies, waits for them, and re-layouts  31.1 us (18%)
  waiting for transfers between devices  26.6 us (16%)
  other arithmetic  9.19 us (5%)
  matrix products  5.24 us (3%)
    all_to_all x2, blocking collectives, copies(): return lax.all_to_all(wide, axis, split_axis=0, concat_axis=0, tiled=True)  21.2 us
    all_to_all x2, blocking collectives, scatter_sum(): got = lax.all_to_all(low, axis, split_axis=0, concat_axis=0, tiled=True)  20.4 us
    ppermute x2, starting transfers between devices, padded_2(): lax.ppermute(head, axis, [((i + 1) % count, i) for i in range(count)])  17 us
    all_to_all x1, starting transfers between devices, on_device(): lax.all_to_all(mixed_grad, TM, split_axis=0, concat_axis=1, tiled=True)  10.3 us
    all_to_all x1, blocking collectives, sum_over_devices(): lax.all_to_all(jnp.stack([rows] * lax.axis_size('core')), 'core', 0, 0)  9.96 us
    all_to_all x1, waiting for transfers between devices, on_device(): lax.all_to_all(mixed_grad, TM, split_axis=0, concat_axis=1, tiled=True)  9.81 us
    ppermute x2, waiting for transfers between devices, padded_2(): lax.ppermute(tail, axis, [(i, (i + 1) % count) for i in range(count)])  9.13 us
    another operation x9, local copies, waits for them, and re-layouts, on_device(): taps_part = jnp.stack(taps_rows, axis=0)  7.22 us
  transfers between devices with their start and end apart: 8, of which 6 were waited for; matrix products, arithmetic and copies ran while one was open for 11% of the time, Pallas kernels for 0%

profile of v1, /device:TPU:1, one launch (start us, length us, event | category | flops | bytes accessed | tf_op | source)
XLA Modules:
  0.0 168.6 jit_solution(1267853126942956874)
XLA Ops:
  3.5 10.3 %all-to-all-start = ((bf16[4,160,256]{2,1,0:T(8,128)(2,1)}), bf16[4,160,256]{2,1,0:T(8,128)(2,1)S(1)}, u32[]{:S(2)}, u32[]{:S(2)}) async-start(bf16[4,160,256]{2,1,0:T(8,128)(2,1)} %add_convert_fusion.1), calls=%async_computation | async-start | bytes 655360 | tf_op jit(solution)/shard_map/all_to_all | solution.py:105
  13.9 9.8 %all-to-all-done = bf16[4,160,256]{2,1,0:T(8,128)(2,1)S(1)} async-done(((bf16[4,160,256]{2,1,0:T(8,128)(2,1)}), bf16[4,160,256]{2,1,0:T(8,128)(2,1)S(1)}, u32[]{:S(2)}, u32[]{:S(2)}) %all-to-all-start) | async-done | bytes 327712 | tf_op jit(solution)/shard_map/all_to_all | solution.py:105
  27.3 11.3 %collective-permute-start.1 = (bf16[20,1,256]{2,0,1:T(8,128)(2,1)S(1)}, bf16[20,1,256]{2,0,1:T(8,128)(2,1)S(1)}, u32[]{:S(2)}, u32[]{:S(2)}) collective-permute-start(bf16[20,1,256]{2,0,1:T(8,128)(2,1)S(1)} %fusion.49), channel_id=1, source_target_pairs={{1,0},{2,1},{3,2},{4,3},{5,4},{6,5},{7,6},{8,7},{9,8},{10,9},{11,1... | collective-permute-start | bytes 30728 | tf_op jit(solution)/shard_map/ppermute | solution.py:26
  39.3 1.9 %collective-permute-start = (bf16[20,1,256]{2,0,1:T(8,128)(2,1)S(1)}, bf16[20,1,256]{2,0,1:T(8,128)(2,1)S(1)}, u32[]{:S(2)}, u32[]{:S(2)}) collective-permute-start(bf16[20,1,256]{2,0,1:T(8,128)(2,1)S(1)} %fusion.48), channel_id=1, source_target_pairs={{0,1},{1,2},{2,3},{3,4},{4,5},{5,6},{6,7},{7,8},{8,9},{9,10},{10,1... | collective-permute-start | bytes 30728 | tf_op jit(solution)/shard_map/ppermute | solution.py:24
  42.3 2.5 %reshape.149 = bf16[640,1024]{1,0:T(8,128)(2,1)S(1)} reshape(bf16[1,2560,256]{2,1,0:T(8,128)(2,1)} %param.16) | data formatting | bytes 2621440 | tf_op jit(solution)/shard_map/reshape | solution.py:72
  46.0 3.7 %collective-permute-done = bf16[20,1,256]{2,0,1:T(8,128)(2,1)S(1)} collective-permute-done((bf16[20,1,256]{2,0,1:T(8,128)(2,1)S(1)}, bf16[20,1,256]{2,0,1:T(8,128)(2,1)S(1)}, u32[]{:S(2)}, u32[]{:S(2)}) %collective-permute-start) | collective-permute-done | bytes 10272 | tf_op jit(solution)/shard_map/ppermute | solution.py:24
  51.6 5.7 %collective-permute-start.3 = (bf16[1,20,1,256]{3,1,2,0:T(8,128)(2,1)S(1)}, bf16[1,20,1,256]{3,1,2,0:T(8,128)(2,1)S(1)}, u32[]{:S(2)}, u32[]{:S(2)}) collective-permute-start(bf16[1,20,1,256]{3,1,2,0:T(8,128)(2,1)S(1)} %copy.128), channel_id=1, source_target_pairs={{1,0},{2,1},{3,2},{4,3},{5,4},{6,5},{7,6},{8,7},{9,8},{10,9},{11,1... | collective-permute-start | bytes 30728 | tf_op jit(solution)/shard_map/ppermute | solution.py:26
  57.3 1.9 %collective-permute-start.2 = (bf16[1,20,1,256]{3,1,2,0:T(8,128)(2,1)S(1)}, bf16[1,20,1,256]{3,1,2,0:T(8,128)(2,1)S(1)}, u32[]{:S(2)}, u32[]{:S(2)}) collective-permute-start(bf16[1,20,1,256]{3,1,2,0:T(8,128)(2,1)S(1)} %copy.127), channel_id=1, source_target_pairs={{0,1},{1,2},{2,3},{3,4},{4,5},{5,6},{6,7},{7,8},{8,9},{9,10},{10,1... | collective-permute-start | bytes 30728 | tf_op jit(solution)/shard_map/ppermute | solution.py:24
  59.2 1.6 convolution_bitcast_fusion
  62.4 5.4 %collective-permute-done.2 = bf16[1,20,1,256]{3,1,2,0:T(8,128)(2,1)S(1)} collective-permute-done((bf16[1,20,1,256]{3,1,2,0:T(8,128)(2,1)S(1)}, bf16[1,20,1,256]{3,1,2,0:T(8,128)(2,1)S(1)}, u32[]{:S(2)}, u32[]{:S(2)}) %collective-permute-start.2) | collective-permute-done | bytes 10272 | tf_op jit(solution)/shard_map/ppermute | solution.py:24
  70.9 2.7 %reduce.8 = bf16[640,256]{1,0:T(8,128)(2,1)S(1)} reduce(bf16[640,1,256]{2,1,0:T(2,128)(2,1)S(1)} %bitcast.115, bf16[]{:T(256)} %broadcast.135), dimensions={1}, to_apply=%bitcast.99.reduce_sub_computation | reduce | bytes 655362
  74.4 6.4 %all-to-all-start.1 = ((bf16[4,2,20480]{2,1,0:T(2,128)(2,1)}), bf16[4,2,20480]{2,1,0:T(2,128)(2,1)S(1)}, u32[]{:S(2)}, u32[]{:S(2)}) async-start(bf16[4,2,20480]{2,1,0:T(2,128)(2,1)} %reshape.204), calls=%async_computation.1 | async-start | bytes 655360 | tf_op jit(solution)/shard_map/all_to_all | solution.py:96
  88.2 2.3 %all-to-all-done.1 = bf16[4,2,20480]{2,1,0:T(2,128)(2,1)S(1)} async-done(((bf16[4,2,20480]{2,1,0:T(2,128)(2,1)}), bf16[4,2,20480]{2,1,0:T(2,128)(2,1)S(1)}, u32[]{:S(2)}, u32[]{:S(2)}) %all-to-all-start.1) | async-done | bytes 327712 | tf_op jit(solution)/shard_map/all_to_all | solution.py:96
  92.0 1.5 convolution_bitcast_fusion.1
  95.2 3.0 %concatenate.24 = f32[1536,256]{0,1:T(8,128)S(1)} concatenate(f32[1024,256]{0,1:T(8,128)S(1)} %copy-done.1, f32[256,256]{0,1:T(8,128)S(1)} %fusion.53, f32[16,256]{0,1:T(8,128)} %copy.113, f32[1,256]{0,1:T(8,128)} %copy.114, f32[1,256]{0,1:T(8,128)} %copy.115, f32[1,256]{0,1:T(8,128)} %copy.116, f32[1,256]{0,1:T(8,128)} %copy.117, f32[1,256]{0,1:T(8,128)} %copy.118, ...), dimensions={0} | concatenate | bytes 3145728 | tf_op jit(solution)/shard_map/concatenate | solution.py:146
  98.3 2.8 %collective-permute-start.4 = (bf16[768,256]{0,1:T(8,128)(2,1)S(1)}, bf16[768,256]{0,1:T(8,128)(2,1)S(1)}, u32[]{:S(2)}, u32[]{:S(2)}) collective-permute-start(bf16[768,256]{0,1:T(8,128)(2,1)S(1)} %dynamic-slice_convert_fusion), channel_id=1, source_target_pairs={{0,128},{128,0},{1,129},{129,1},{2,130},{130,2},{3,131},{131,3},{4... | collective-permute-start | bytes 1179656 | tf_op jit(solution)/shard_map/ppermute | solution.py:51
  102.7 10.2 %all_to_all.51 = bf16[4,192,256]{2,1,0:T(8,128)(2,1)S(1)} all-to-all(bf16[4,192,256]{2,1,0:T(8,128)(2,1)S(1)} %bitcast.117), channel_id=1, replica_groups=mesh['yh'=2,'core'=2,'x'=4,'z'=8,'yl'=4] {'x'}, dimensions={0} | all-to-all | bytes 786432 | tf_op jit(solution)/shard_map/all_to_all | solution.py:36
  113.0 10.2 %all_to_all.52 = bf16[8,24,256]{2,1,0:T(8,128)(2,1)S(1)} all-to-all(bf16[8,24,256]{2,1,0:T(8,128)(2,1)S(1)} %bitcast.122), channel_id=1, replica_groups=mesh['yh'=2,'core'=2,'x'=4,'z'=8,'yl'=4] {'z'}, dimensions={0} | all-to-all | bytes 196608 | tf_op jit(solution)/shard_map/all_to_all | solution.py:36
  123.2 11.2 %all_to_all.53 = bf16[8,24,256]{2,1,0:T(8,128)(2,1)S(1)} all-to-all(bf16[8,24,256]{2,1,0:T(8,128)(2,1)S(1)} %broadcast_in_dim.50), channel_id=1, replica_groups=mesh['yh'=2,'core'=2,'x'=4,'z'=8,'yl'=4] {'yh','yl'}, dimensions={0} | all-to-all | bytes 196608 | tf_op jit(solution)/shard_map/all_to_all | solution.py:43
  134.5 10.0 %all_to_all.54 = bf16[8,24,256]{2,1,0:T(8,128)(2,1)S(1)} all-to-all(bf16[8,24,256]{2,1,0:T(8,128)(2,1)S(1)} %broadcast_in_dim.51), channel_id=1, replica_groups=mesh['yh'=2,'core'=2,'x'=4,'z'=8,'yl'=4] {'z'}, dimensions={0} | all-to-all | bytes 196608 | tf_op jit(solution)/shard_map/all_to_all | solution.py:43
  145.2 3.5 %all-to-all-start.6 = ((bf16[4,192,256]{2,1,0:T(8,128)(2,1)}), bf16[4,192,256]{2,1,0:T(8,128)(2,1)S(1)}, u32[]{:S(2)}, u32[]{:S(2)}) async-start(bf16[4,192,256]{2,1,0:T(8,128)(2,1)} %broadcast_in_dim.53), calls=%async_computation.6 | async-start | bytes 786432 | tf_op jit(solution)/shard_map/all_to_all | solution.py:43
  149.2 1.6 reshape.150
  150.9 4.0 %all-to-all-done.6 = bf16[4,192,256]{2,1,0:T(8,128)(2,1)S(1)} async-done(((bf16[4,192,256]{2,1,0:T(8,128)(2,1)}), bf16[4,192,256]{2,1,0:T(8,128)(2,1)S(1)}, u32[]{:S(2)}, u32[]{:S(2)}) %all-to-all-start.6) | async-done | bytes 393248 | tf_op jit(solution)/shard_map/all_to_all | solution.py:43
  154.9 10.0 %all_to_all.55 = bf16[2,768,256]{2,1,0:T(8,128)(2,1)S(1)} all-to-all(bf16[2,768,256]{2,1,0:T(8,128)(2,1)S(1)} %pad_maximum_fusion), channel_id=1, replica_groups=mesh['yh'=2,'core'=2,'x'=4,'z'=8,'yl'=4] {'core'}, dimensions={0} | all-to-all | bytes 1572864 | tf_op jit(solution)/shard_map/all_to_all | solution.py:60
  (120 shorter events, 33.9 us)
Async XLA Ops:
  0.6 50.1 %copy-start = (bf16[1024,256]{1,0:T(8,128)(2,1)S(1)}, bf16[1024,256]{1,0:T(8,128)(2,1)}, u32[]{:S(2)}) copy-start(bf16[1024,256]{1,0:T(8,128)(2,1)} %param.17) | copy-start | bytes 1572868
  2.5 11.3 %copy-start.20 = (s32[1,2,20]{2,1,0:T(2,128)S(1)}, s32[1,2,20]{2,1,0:T(2,128)}, u32[]{:S(2)}) copy-start(s32[1,2,20]{2,1,0:T(2,128)} %param.22) | copy-start | bytes 484
  2.5 11.3 %copy-start.19 = (f32[9,256]{1,0:T(8,128)S(1)}, f32[9,256]{1,0:T(8,128)}, u32[]{:S(2)}) copy-start(f32[9,256]{1,0:T(8,128)} %param.19) | copy-start | bytes 27652
  2.5 21.2 %copy-start.7 = (bf16[256,256]{1,0:T(8,128)(2,1)S(1)}, bf16[256,256]{1,0:T(8,128)(2,1)}, u32[]{:S(2)}) copy-start(bf16[256,256]{1,0:T(8,128)(2,1)} %param.20) | copy-start | bytes 393220
  3.5 20.2 %all-to-all-start = ((bf16[4,160,256]{2,1,0:T(8,128)(2,1)}), bf16[4,160,256]{2,1,0:T(8,128)(2,1)S(1)}, u32[]{:S(2)}, u32[]{:S(2)}) async-start(bf16[4,160,256]{2,1,0:T(8,128)(2,1)} %add_convert_fusion.1), calls=%async_computation | async-start | bytes 655360 | tf_op jit(solution)/shard_map/all_to_all | solution.py:105
  13.8 10.5 %copy-start.13 = (f32[1,256]{1,0:T(1,128)}, f32[1,256]{1,0:T(1,128)S(1)}, u32[]{:S(2)}) copy-start(f32[1,256]{1,0:T(1,128)S(1)} %get-tuple-element.66) | copy-start | bytes 3076
  13.8 10.5 %copy-start.15 = (f32[1,256]{1,0:T(1,128)}, f32[1,256]{1,0:T(1,128)S(1)}, u32[]{:S(2)}) copy-start(f32[1,256]{1,0:T(1,128)S(1)} %get-tuple-element.67) | copy-start | bytes 3076
  13.8 10.5 %copy-start.17 = (f32[1,256]{1,0:T(1,128)}, f32[1,256]{1,0:T(1,128)S(1)}, u32[]{:S(2)}) copy-start(f32[1,256]{1,0:T(1,128)S(1)} %get-tuple-element.68) | copy-start | bytes 3076
  23.7 27.1 %copy-start.2 = (bf16[4,160,256]{2,1,0:T(8,128)(2,1)}, bf16[4,160,256]{2,1,0:T(8,128)(2,1)S(1)}, u32[]{:S(2)}) copy-start(bf16[4,160,256]{2,1,0:T(8,128)(2,1)S(1)} %all-to-all-done) | copy-start | bytes 983044
  24.4 16.9 %copy-start.4 = (bf16[4,160,256]{2,1,0:T(8,128)(2,1)S(1)}, bf16[4,160,256]{2,1,0:T(8,128)(2,1)}, u32[]{:S(2)}) copy-start(bf16[4,160,256]{2,1,0:T(8,128)(2,1)} %param.23) | copy-start | bytes 983044
  27.3 18.7 %collective-permute-start.1 = (bf16[20,1,256]{2,0,1:T(8,128)(2,1)S(1)}, bf16[20,1,256]{2,0,1:T(8,128)(2,1)S(1)}, u32[]{:S(2)}, u32[]{:S(2)}) collective-permute-start(bf16[20,1,256]{2,0,1:T(8,128)(2,1)S(1)} %fusion.49), channel_id=1, source_target_pairs={{1,0},{2,1},{3,2},{4,3},{5,4},{6,5},{7,6},{8,7},{9,8},{10,9},{11,1... | collective-permute-start | bytes 30728 | tf_op jit(solution)/shard_map/ppermute | solution.py:26
  39.3 10.4 %collective-permute-start = (bf16[20,1,256]{2,0,1:T(8,128)(2,1)S(1)}, bf16[20,1,256]{2,0,1:T(8,128)(2,1)S(1)}, u32[]{:S(2)}, u32[]{:S(2)}) collective-permute-start(bf16[20,1,256]{2,0,1:T(8,128)(2,1)S(1)} %fusion.48), channel_id=1, source_target_pairs={{0,1},{1,2},{2,3},{3,4},{4,5},{5,6},{6,7},{7,8},{8,9},{9,10},{10,1... | collective-permute-start | bytes 30728 | tf_op jit(solution)/shard_map/ppermute | solution.py:24
  51.6 9.2 %copy-start.5 = (bf16[640,256]{1,0:T(8,128)(2,1)}, bf16[640,256]{1,0:T(8,128)(2,1)S(1)}, u32[]{:S(2)}) copy-start(bf16[640,256]{1,0:T(8,128)(2,1)S(1)} %get-tuple-element.53) | copy-start | bytes 983044
  51.6 10.1 %collective-permute-start.3 = (bf16[1,20,1,256]{3,1,2,0:T(8,128)(2,1)S(1)}, bf16[1,20,1,256]{3,1,2,0:T(8,128)(2,1)S(1)}, u32[]{:S(2)}, u32[]{:S(2)}) collective-permute-start(bf16[1,20,1,256]{3,1,2,0:T(8,128)(2,1)S(1)} %copy.128), channel_id=1, source_target_pairs={{1,0},{2,1},{3,2},{4,3},{5,4},{6,5},{7,6},{8,7},{9,8},{10,9},{11,1... | collective-permute-start | bytes 30728 | tf_op jit(solution)/shard_map/ppermute | solution.py:26
  57.3 10.5 %collective-permute-start.2 = (bf16[1,20,1,256]{3,1,2,0:T(8,128)(2,1)S(1)}, bf16[1,20,1,256]{3,1,2,0:T(8,128)(2,1)S(1)}, u32[]{:S(2)}, u32[]{:S(2)}) collective-permute-start(bf16[1,20,1,256]{3,1,2,0:T(8,128)(2,1)S(1)} %copy.127), channel_id=1, source_target_pairs={{0,1},{1,2},{2,3},{3,4},{4,5},{5,6},{6,7},{7,8},{8,9},{9,10},{10,1... | collective-permute-start | bytes 30728 | tf_op jit(solution)/shard_map/ppermute | solution.py:24
  60.8 7.9 %copy-start.14 = (f32[1,256]{1,0:T(1,128)S(1)}, f32[1,256]{1,0:T(1,128)}, u32[]{:S(2)}) copy-start(f32[1,256]{1,0:T(1,128)} %copy-done.13) | copy-start | bytes 3076
  60.8 8.0 %copy-start.16 = (f32[1,256]{1,0:T(1,128)S(1)}, f32[1,256]{1,0:T(1,128)}, u32[]{:S(2)}) copy-start(f32[1,256]{1,0:T(1,128)} %copy-done.15) | copy-start | bytes 3076
  60.8 8.0 %copy-start.18 = (f32[1,256]{1,0:T(1,128)S(1)}, f32[1,256]{1,0:T(1,128)}, u32[]{:S(2)}) copy-start(f32[1,256]{1,0:T(1,128)} %copy-done.17) | copy-start | bytes 3076
  70.3 10.4 %copy-start.10 = (bf16[20,1,256]{2,1,0:T(2,128)(2,1)S(1)}, bf16[20,1,256]{2,1,0:T(2,128)(2,1)}, u32[]{:S(2)}) copy-start(bf16[20,1,256]{2,1,0:T(2,128)(2,1)} %copy-done.9) | copy-start | bytes 30724
  70.3 10.4 %copy-start.12 = (bf16[20,1,256]{2,1,0:T(2,128)(2,1)S(1)}, bf16[20,1,256]{2,1,0:T(2,128)(2,1)}, u32[]{:S(2)}) copy-start(bf16[20,1,256]{2,1,0:T(2,128)(2,1)} %copy-done.11) | copy-start | bytes 30724
  74.4 16.2 %all-to-all-start.1 = ((bf16[4,2,20480]{2,1,0:T(2,128)(2,1)}), bf16[4,2,20480]{2,1,0:T(2,128)(2,1)S(1)}, u32[]{:S(2)}, u32[]{:S(2)}) async-start(bf16[4,2,20480]{2,1,0:T(2,128)(2,1)} %reshape.204), calls=%async_computation.1 | async-start | bytes 655360 | tf_op jit(solution)/shard_map/all_to_all | solution.py:96
  98.3 4.1 %collective-permute-start.4 = (bf16[768,256]{0,1:T(8,128)(2,1)S(1)}, bf16[768,256]{0,1:T(8,128)(2,1)S(1)}, u32[]{:S(2)}, u32[]{:S(2)}) collective-permute-start(bf16[768,256]{0,1:T(8,128)(2,1)S(1)} %dynamic-slice_convert_fusion), channel_id=1, source_target_pairs={{0,128},{128,0},{1,129},{129,1},{2,130},{130,2},{3,131},{131,3},{4... | collective-permute-start | bytes 1179656 | tf_op jit(solution)/shard_map/ppermute | solution.py:51
  112.9 35.7 %copy-start.6 = (bf16[640,256]{1,0:T(8,128)(2,1)S(1)}, bf16[640,256]{1,0:T(8,128)(2,1)}, u32[]{:S(2)}) copy-start(bf16[640,256]{1,0:T(8,128)(2,1)} %copy-done.5) | copy-start | bytes 983044
  145.2 9.7 %all-to-all-start.6 = ((bf16[4,192,256]{2,1,0:T(8,128)(2,1)}), bf16[4,192,256]{2,1,0:T(8,128)(2,1)S(1)}, u32[]{:S(2)}, u32[]{:S(2)}) async-start(bf16[4,192,256]{2,1,0:T(8,128)(2,1)} %broadcast_in_dim.53), calls=%async_computation.6 | async-start | bytes 786432 | tf_op jit(solution)/shard_map/all_to_all | solution.py:43
  (6 other events, 22.2 us)
